TPU v7x, 128 devices: a whole 4x4x4 slice. The times are simulated.
128 devices in a mesh: dp: 16 (over z, y), tensor: 8 (over x, core).
Axes of the slice: x: 4, y: 4, z: 4, core: 2. Of those that a mesh axis runs over, the one named last changes fastest.
Arguments:
- dense: bfloat16 [3072, 2048], P('dp'), may hold values from -8 to 8
- bottom_weight: bfloat16 [2048, 16384], P(None, 'tensor'), may hold values from -0.125 to 0.125
- bottom_bias: float32 [16384], P('tensor'), may hold values from -3 to 3
- cross_blocks: bfloat16 [80, 512, 512], P('tensor', 'dp'), may hold values from -0.25 to 0.25
- cross_bias: float32 [16384], P('tensor'), may hold values from -3 to 3
- cotangent: bfloat16 [3072, 16384], P('dp', 'tensor'), may hold values from -6 to 6
- in_blocks: int32 [8, 10], replicated, may hold values from 0 to 31, as said below
- out_blocks: int32 [8, 10], replicated, may hold values from 0 to 31, as said below
- live_slots: int32 [8], replicated, may hold values from 2 to 10, as said below
Outputs:
- cross_out: bfloat16 [3072, 16384], P('dp', 'tensor')
- grad_bottom: float32 [2048, 16384], P('dp', 'tensor')
- grad_bias_bottom: float32 [16384], P('tensor')
- grad_blocks: float32 [80, 512, 512], P('tensor', 'dp')
- grad_bias: float32 [16384], P('tensor')
Inputs may be any that keep to these rules, and one draw needn't show every extreme that they name: `in_blocks`: among the live slots of one tensor device, at most 2 have input blocks held by any one tensor device (blocks s * 16384 / (512 * 8) onward for device s), and this most is reached in every draw. `out_blocks`: among the live slots of one tensor device, at most 2 have output blocks held by any one tensor device, and this most is reached in every draw. `live_slots`: some tensor device has all 10 slots live.
All inputs are finite; a program needn't handle non-finite values.
Results may differ from a plain program's by a relative error of at most 0.014.
Values may be sent and summed in bfloat16 or wider, within the bound.
A program may use at most 128 MiB of HBM per device.

v0:
```python
import jax
import jax.numpy as jnp
from jax import lax
from jax.sharding import PartitionSpec as P

BLK = 512
SLOTS = 10


def slot_ranks(owner, alive):
    order = jnp.arange(owner.shape[1])
    earlier = order[None, :] < order[:, None]
    same = (owner[:, :, None] == owner[:, None, :]) & alive[:, None, :] & earlier[None, :, :]
    return jnp.sum(same.astype(jnp.int32), axis=2)


def post_table(owner_mine, rank_mine, alive_mine, groups, capacity):
    slot_count = owner_mine.shape[0]
    match = (
        (owner_mine[None, None, :] == jnp.arange(groups)[:, None, None])
        & (rank_mine[None, None, :] == jnp.arange(capacity)[None, :, None])
        & alive_mine[None, None, :]
    )
    chosen = jnp.sum(match.astype(jnp.int32) * jnp.arange(slot_count)[None, None, :], axis=2)
    filled = jnp.any(match, axis=2)
    return (chosen, filled)


def pack_parts(parts, chosen, filled):
    picked = jnp.take(parts, chosen.reshape(-1), axis=1) * filled.reshape(-1)[None, :, None].astype(
        parts.dtype
    )
    return picked.reshape(parts.shape[0], chosen.shape[0], chosen.shape[1] * parts.shape[2])


def collect_parts(received, owner, local, rank, alive, target, capacity, per_device):
    row_count, groups, span_width = received.shape
    block_width = span_width // capacity
    match = ((owner == target) & alive)[:, :, None] & (
        rank[:, :, None] == jnp.arange(capacity)[None, None, :]
    )
    matches = match[:, :, :, None] & (
        local[:, :, None, None] == jnp.arange(per_device)[None, None, None, :]
    )
    onehot = (
        jnp.sum(matches.astype(jnp.int32), axis=1)
        .reshape(groups * capacity, per_device)
        .astype(jnp.bfloat16)
    )
    flattened = received.reshape(row_count, groups * capacity, block_width)
    summed = jnp.einsum("rib,il->rlb", flattened, onehot, preferred_element_type=jnp.float32)
    return summed.reshape(row_count, per_device * block_width)


def on_device(
    dense,
    bottom_weight,
    bottom_bias,
    cross_blocks,
    cross_bias,
    cotangent,
    in_blocks,
    out_blocks,
    live_slots,
):
    groups = lax.axis_size("tensor")
    mine = lax.axis_index("tensor")
    row_count = dense.shape[0]
    local_width = bottom_weight.shape[1]
    per_device = local_width // BLK
    capacity = -(-SLOTS // groups)
    preact = jnp.dot(dense, bottom_weight, preferred_element_type=jnp.float32) + bottom_bias
    start = jax.nn.silu(preact).astype(jnp.bfloat16)
    start_wide = start.astype(jnp.float32)
    cot_wide = cotangent.astype(jnp.float32)
    grad_mixed = cot_wide * start_wide
    grad_mixed_low = grad_mixed.astype(jnp.bfloat16)
    alive = jnp.arange(SLOTS)[None, :] < live_slots[:, None]
    alive_mine = alive[mine]
    switch = alive_mine.astype(jnp.bfloat16)[None, :, None]
    in_owner = in_blocks // per_device
    in_local = in_blocks % per_device
    out_owner = out_blocks // per_device
    out_local = out_blocks % per_device
    in_rank = slot_ranks(in_owner, alive)
    out_rank = slot_ranks(out_owner, alive)
    whole_start = lax.all_gather(start, "tensor", axis=1, tiled=True)
    fetched = jnp.take(whole_start.reshape(row_count, -1, BLK), in_blocks[mine], axis=1)
    taken = fetched
    product = jnp.einsum(
        "rki,kij->rkj",
        taken,
        lax.all_gather(cross_blocks, "dp", axis=1, tiled=True),
        preferred_element_type=jnp.float32,
    )
    parts = product.astype(jnp.bfloat16) * switch
    chosen_out, filled_out = post_table(
        out_owner[mine], out_rank[mine], alive_mine, groups, capacity
    )
    arrived_parts = lax.all_to_all(
        pack_parts(parts, chosen_out, filled_out), "tensor", split_axis=1, concat_axis=1, tiled=True
    )
    mixed = (
        collect_parts(
            arrived_parts, out_owner, out_local, out_rank, alive, mine, capacity, per_device
        )
        + cross_bias
    )
    cross_out = (start_wide * mixed + start_wide).astype(jnp.bfloat16)
    whole_grad = lax.all_gather(grad_mixed_low, "tensor", axis=1, tiled=True)
    upstream = jnp.take(whole_grad.reshape(row_count, -1, BLK), out_blocks[mine], axis=1)
    upstream = upstream * switch
    backward = jnp.einsum(
        "rkj,kij->rki",
        upstream,
        lax.all_gather(cross_blocks, "dp", axis=1, tiled=True),
        preferred_element_type=jnp.float32,
    )
    back_parts = backward.astype(jnp.bfloat16)
    chosen_in, filled_in = post_table(in_owner[mine], in_rank[mine], alive_mine, groups, capacity)
    arrived_back = lax.all_to_all(
        pack_parts(back_parts, chosen_in, filled_in),
        "tensor",
        split_axis=1,
        concat_axis=1,
        tiled=True,
    )
    grad_start = collect_parts(
        arrived_back, in_owner, in_local, in_rank, alive, mine, capacity, per_device
    )
    block_terms = jnp.einsum("rki,rkj->kij", fetched, upstream, preferred_element_type=jnp.float32)
    grad_blocks = lax.psum_scatter(
        block_terms.astype(jnp.bfloat16), "dp", scatter_dimension=1, tiled=True
    ).astype(jnp.float32)
    grad_start = grad_start + cot_wide * mixed + cot_wide
    sigma = jax.nn.sigmoid(preact)
    grad_pre = grad_start * sigma * (1.0 + preact * (1.0 - sigma))
    grad_pre_low = grad_pre.astype(jnp.bfloat16)
    taken = dense
    grad_bottom = lax.psum_scatter(
        lax.dot_general(
            taken, grad_pre_low, (((0,), (0,)), ((), ())), preferred_element_type=jnp.float32
        ).astype(jnp.bfloat16),
        "dp",
        scatter_dimension=0,
        tiled=True,
    ).astype(jnp.float32)
    bias_sums = lax.psum((jnp.sum(grad_pre, axis=0), jnp.sum(grad_mixed, axis=0)), "dp")
    return (cross_out, grad_bottom, bias_sums[0], grad_blocks, bias_sums[1])


def solution(mesh):
    return jax.shard_map(
        on_device,
        mesh=mesh,
        in_specs=(
            P("dp", None),
            P(None, "tensor"),
            P("tensor"),
            P("tensor", "dp", None),
            P("tensor"),
            P("dp", "tensor"),
            P(),
            P(),
            P(),
        ),
        out_specs=(
            P("dp", "tensor"),
            P("dp", "tensor"),
            P("tensor"),
            P("tensor", "dp", None),
            P("tensor"),
        ),
        check_vma=False,
    )
```

profile of v0, /device:TPU:0, one launch (start us, length us, event | category | flops | bytes accessed | tf_op | source)
XLA Modules:
  0.0 400.9 jit_solution(8510571627176802936)
XLA Ops:
  8.3 7.8 %fusion.9 = (f32[2048]{0:T(1024)}, bf16[192,2048]{1,0:T(8,128)(2,1)}, f32[192,2048]{1,0:T(8,128)}) fusion(bf16[192,2048]{1,0:T(8,128)(2,1)} %param.18, f32[2048]{0:T(1024)} %param.15, bf16[192,2048]{1,0:T(8,128)(2,1)S(1)} %copy-done, bf16[2048,2048]{1,0:T(8,128)(2,1)} %param.14), kind=kOutput, calls=%fused_computation.28 | convolution fusion | flops 1614542848 | bytes 12337152 | tf_op jit(solution)/shard_map/dot_general | solution.py:72
  21.2 38.5 %all-gather.4.cloned.1.call-done = bf16[192,16384]{1,0:T(8,128)(2,1)} async-done(((bf16[192,2048]{1,0:T(8,128)(2,1)}), bf16[192,16384]{1,0:T(8,128)(2,1)}) %all-gather.4.cloned.1.call-update) | async-done | bytes 6291472 | tf_op jit(solution)/shard_map/all_gather | solution.py:87
  59.6 6.2 %copy.90 = bf16[24,32,8,512]{3,2,0,1:T(8,128)(2,1)} copy(bf16[24,32,8,512]{3,2,1,0:T(8,128)(2,1)} %bitcast.71) | data formatting | bytes 12582912 | tf_op jit(solution)/shard_map/reshape | solution.py:88
  65.8 37.0 %all-gather.8.cloned.1.call-done = bf16[192,16384]{1,0:T(8,128)(2,1)} async-done(((bf16[192,2048]{1,0:T(8,128)(2,1)}), bf16[192,16384]{1,0:T(8,128)(2,1)}) %all-gather.8.cloned.1.call-update) | async-done | bytes 6291472 | tf_op jit(solution)/shard_map/all_gather | solution.py:110
  102.9 6.3 %copy.89 = bf16[24,32,8,512]{3,2,0,1:T(8,128)(2,1)} copy(bf16[24,32,8,512]{3,2,1,0:T(8,128)(2,1)} %bitcast.72) | data formatting | bytes 12582912 | tf_op jit(solution)/shard_map/reshape | solution.py:111
  109.2 4.9 %gather_fusion = bf16[10,192,512]{2,1,0:T(8,128)(2,1)} fusion(bf16[192,32,512]{2,0,1:T(8,128)(2,1)} %bitcast.69, s32[1024]{0:T(1024)S(1)} %pad_clamp_fusion.3), kind=kCustom, calls=%fused_computation.clone | custom fusion | bytes 3932200 | tf_op jit(solution)/shard_map/jit(_take)/gather | solution.py:88
  114.0 3.7 gather_fusion.2
  117.8 5.8 %convolution_convert_fusion = bf16[10,512,512]{2,1,0:T(8,128)(2,1)} fusion(bf16[10,192,512]{2,1,0:T(8,128)(2,1)} %gather_fusion, pred[10]{0:T(512)(128)(4,1)} %get-tuple-element.65, bf16[10,192,512]{2,1,0:T(8,128)(2,1)S(1)} %gather_fusion.2, pred[10]{0:T(512)(128)(4,1)S(1)} %get-tuple-element.44, bf16[10]{0:T(256)(128)(2,1)} %get-tuple-element.50), kind=kOutput, calls=%fused_computation.9 | convolution fusion | flops 1012203520 | bytes 9175080 | tf_op jit(solution)/shard_map/rki,rkj->kij/dot_general | solution.py:131
  138.9 22.7 %all-gather.6.cloned.1.call-done = bf16[10,512,512]{2,1,0:T(8,128)(2,1)} async-done(((bf16[10,32,512]{2,1,0:T(8,128)(2,1)}), bf16[10,512,512]{2,1,0:T(8,128)(2,1)}) %all-gather.6.cloned.1.call-update) | async-done | bytes 5242896 | tf_op jit(solution)/shard_map/all_gather | solution.py:93
  161.6 5.7 %multiply_bitcast_fusion = bf16[192,10,512]{2,0,1:T(8,128)(2,1)} fusion(bf16[10,512,512]{2,1,0:T(8,128)(2,1)} %all-gather.6.cloned.1.call-done, bf16[10]{0:T(256)(128)(2,1)} %get-tuple-element.50, bf16[10,192,512]{2,1,0:T(8,128)(2,1)} %gather_fusion, pred[10]{0:T(512)(128)(4,1)} %get-tuple-element.65), kind=kOutput, calls=%fused_computation.20 | convolution fusion | flops 1009582080 | bytes 9175070 | tf_op jit(solution)/shard_map/rki,kij->rkj/dot_general | solution.py:90
  167.3 4.0 %gather_fusion.1 = bf16[16,192,512]{2,1,0:T(8,128)(2,1)} fusion(bf16[192,10,512]{2,0,1:T(8,128)(2,1)} %multiply_bitcast_fusion, s32[1024]{0:T(1024)} %pad_clamp_fusion.2), kind=kCustom, calls=%fused_computation.1.clone | custom fusion | bytes 6291520 | tf_op jit(solution)/shard_map/jit(_take)/gather | solution.py:30
  173.6 3.4 copy.62
  177.1 5.7 %reshape.254 = bf16[192,8,1024]{2,1,0:T(8,128)(2,1)} reshape(bf16[192,16,512]{2,1,0:T(8,128)(2,1)} %copy.62) | data formatting | bytes 6291456 | tf_op jit(solution)/shard_map/reshape | solution.py:33
  182.8 5.4 %copy.63 = bf16[192,8,1024]{2,0,1:T(8,128)(2,1)} copy(bf16[192,8,1024]{2,1,0:T(8,128)(2,1)} %reshape.254) | data formatting | bytes 6291456 | tf_op jit(solution)/shard_map/reshape | solution.py:33
  188.1 4.6 %all-to-all-start = ((bf16[192,8,1024]{2,0,1:T(8,128)(2,1)}), bf16[192,8,1024]{2,0,1:T(8,128)(2,1)}, u32[]{:S(2)}, u32[]{:S(2)}) async-start(bf16[192,8,1024]{2,0,1:T(8,128)(2,1)} %copy.63), calls=%async_computation | async-start | bytes 6291456 | tf_op jit(solution)/shard_map/all_to_all | solution.py:100
  201.6 5.8 %convert_bitcast_fusion.1 = bf16[192,10,512]{2,0,1:T(8,128)(2,1)} fusion(bf16[10,512,512]{2,1,0:T(8,128)(2,1)} %all-gather.6.cloned.1.call-done, bf16[10,192,512]{2,1,0:T(8,128)(2,1)S(1)} %gather_fusion.2, pred[10]{0:T(512)(128)(4,1)} %copy-done.21, bf16[10]{0:T(256)(128)(2,1)} %get-tuple-element.50), kind=kOutput, calls=%fused_computation.19 | convolution fusion | flops 1009582080 | bytes 9175070 | tf_op jit(solution)/shard_map/rkj,kij->rki/dot_general | solution.py:113
  207.4 4.1 %gather_fusion.3 = bf16[16,192,512]{2,1,0:T(8,128)(2,1)} fusion(bf16[192,10,512]{2,0,1:T(8,128)(2,1)} %convert_bitcast_fusion.1, s32[1024]{0:T(1024)} %pad_clamp_fusion), kind=kCustom, calls=%fused_computation.3.clone | custom fusion | bytes 6291520 | tf_op jit(solution)/shard_map/jit(_take)/gather | solution.py:30
  213.8 3.5 copy.72
  217.3 5.7 %reshape.259 = bf16[192,8,1024]{2,1,0:T(8,128)(2,1)} reshape(bf16[192,16,512]{2,1,0:T(8,128)(2,1)} %copy.72) | data formatting | bytes 6291456 | tf_op jit(solution)/shard_map/reshape | solution.py:33
  223.0 5.3 %copy.73 = bf16[192,8,1024]{2,0,1:T(8,128)(2,1)} copy(bf16[192,8,1024]{2,1,0:T(8,128)(2,1)} %reshape.259) | data formatting | bytes 6291456 | tf_op jit(solution)/shard_map/reshape | solution.py:33
  228.3 2.9 all-to-all-done
  231.2 4.4 %all-to-all-start.1 = ((bf16[192,8,1024]{2,0,1:T(8,128)(2,1)}), bf16[192,8,1024]{2,0,1:T(8,128)(2,1)}, u32[]{:S(2)}, u32[]{:S(2)}) async-start(bf16[192,8,1024]{2,0,1:T(8,128)(2,1)} %copy.73), calls=%async_computation.1 | async-start | bytes 6291456 | tf_op jit(solution)/shard_map/all_to_all | solution.py:121
  236.6 5.3 %copy.64 = bf16[192,8,1024]{2,1,0:T(8,128)(2,1)} copy(bf16[192,8,1024]{2,0,1:T(8,128)(2,1)} %all-to-all-done) | data formatting | bytes 6291456 | tf_op jit(solution)/shard_map/all_to_all | solution.py:100
  241.9 5.7 %reshape.255 = bf16[192,16,512]{2,1,0:T(8,128)(2,1)} reshape(bf16[192,8,1024]{2,1,0:T(8,128)(2,1)} %copy.64) | data formatting | bytes 6291456 | tf_op jit(solution)/shard_map/reshape | solution.py:50
  250.7 23.4 %all-to-all-done.1 = bf16[192,8,1024]{2,0,1:T(8,128)(2,1)} async-done(((bf16[192,8,1024]{2,0,1:T(8,128)(2,1)}), bf16[192,8,1024]{2,0,1:T(8,128)(2,1)}, u32[]{:S(2)}, u32[]{:S(2)}) %all-to-all-start.1) | async-done | bytes 3145760 | tf_op jit(solution)/shard_map/all_to_all | solution.py:121
  274.0 5.2 %copy.74 = bf16[192,8,1024]{2,1,0:T(8,128)(2,1)} copy(bf16[192,8,1024]{2,0,1:T(8,128)(2,1)} %all-to-all-done.1) | data formatting | bytes 6291456 | tf_op jit(solution)/shard_map/all_to_all | solution.py:121
  279.3 5.6 %reshape.260 = bf16[192,16,512]{2,1,0:T(8,128)(2,1)} reshape(bf16[192,8,1024]{2,1,0:T(8,128)(2,1)} %copy.74) | data formatting | bytes 6291456 | tf_op jit(solution)/shard_map/reshape | solution.py:50
  284.9 2.5 fusion.30
  290.9 5.6 %convert_bitcast_fusion = bf16[2048,2048]{0,1:T(8,128)(2,1)} fusion(bf16[192,2048]{1,0:T(8,128)(2,1)S(1)} %copy-done, bf16[192,2048]{1,0:T(8,128)(2,1)S(1)} %get-tuple-element.43), kind=kOutput, calls=%fused_computation.4 | convolution fusion | flops 1614807040 | bytes 9961472 | tf_op jit(solution)/shard_map/dot_general | solution.py:141
  296.6 12.3 %copy.81 = bf16[2048,2048]{1,0:T(8,128)(2,1)} copy(bf16[2048,2048]{0,1:T(8,128)(2,1)} %convert_bitcast_fusion) | data formatting | bytes 16777216
  309.5 72.9 %all-reduce = (f32[2048]{0:T(1024)}, f32[2048]{0:T(1024)}) all-reduce(f32[2048]{0:T(1024)S(1)} %get-tuple-element.42, f32[2048]{0:T(1024)S(1)} %copy-done.10), channel_id=1, replica_groups=mesh['dp'=16,'tensor'=8] {'dp'}, use_global_device_ids=true, to_apply=%region_10.13 | all-reduce | flops 4096 | bytes 32768 | tf_op jit(solution)/shard_map/psum | solution.py:148
  384.3 7.5 %reduce-scatter.7.cloned.1.call-done = bf16[128,2048]{1,0:T(8,128)(2,1)} async-done(((bf16[2048,2048]{1,0:T(8,128)(2,1)}), bf16[128,2048]{1,0:T(8,128)(2,1)}) %reduce-scatter.7.cloned.1.call-update) | async-done | bytes 524304
  (113 shorter events, 47.3 us)
Async XLA Ops:
  7.2 1.1 copy-start
  7.2 9.0 %copy-start.2 = (bf16[192,2048]{1,0:T(8,128)(2,1)S(1)}, bf16[192,2048]{1,0:T(8,128)(2,1)}, u32[]{:S(2)}) copy-start(bf16[192,2048]{1,0:T(8,128)(2,1)} %param.18) | copy-start | bytes 2359300
  7.2 52.4 %all-gather.4.cloned.1.call-start = ((), (), s32[]{:S(2)}) async-start(), calls=%async_computation.4 | async-start | bytes 7077888 | tf_op jit(solution)/shard_map/all_gather | solution.py:87
  16.1 3.2 copy-start.6
  16.1 3.2 copy-start.8
  16.1 3.2 copy-start.20
  16.1 86.8 %all-gather.8.cloned.1.call-start = ((), (), s32[]{:S(2)}) async-start(), calls=%async_computation.6 | async-start | bytes 7077888 | tf_op jit(solution)/shard_map/all_gather | solution.py:110
  18.5 143.1 %all-gather.6.cloned.1.call-start = ((), (), s32[]{:S(2)}) async-start(), calls=%async_computation.5 | async-start | bytes 5570560 | tf_op jit(solution)/shard_map/all_gather | solution.py:93
  19.2 363.2 %reduce-scatter.5.cloned.1.call-start = ((), (), s32[]{:S(2)}) async-start(), calls=%async_computation.7 | async-start | bytes 5570560 | tf_op jit(solution)/shard_map/reduce_scatter | solution.py:132
  20.0 45.9 %copy-start.12 = (pred[8,10]{1,0:T(8,128)(4,1)}, pred[8,10]{1,0:T(8,128)(4,1)S(1)}, u32[]{:S(2)}) copy-start(pred[8,10]{1,0:T(8,128)(4,1)S(1)} %get-tuple-element.57) | copy-start | bytes 244
  20.0 103.6 %copy-start.4 = (s32[8,10]{1,0:T(8,128)}, s32[8,10]{1,0:T(8,128)S(1)}, u32[]{:S(2)}) copy-start(s32[8,10]{1,0:T(8,128)S(1)} %get-tuple-element.53) | copy-start | bytes 964
  20.0 104.3 %copy-start.5 = (s32[8,10]{1,0:T(8,128)}, s32[8,10]{1,0:T(8,128)S(1)}, u32[]{:S(2)}) copy-start(s32[8,10]{1,0:T(8,128)S(1)} %get-tuple-element.56) | copy-start | bytes 964
  21.1 96.6 %copy-start.21 = (pred[10]{0:T(512)(128)(4,1)}, pred[10]{0:T(512)(128)(4,1)S(1)}, u32[]{:S(2)}) copy-start(pred[10]{0:T(512)(128)(4,1)S(1)} %get-tuple-element.44) | copy-start | bytes 34
  127.1 2.0 copy-start.17
  127.1 2.0 copy-start.18
  127.1 0.6 copy-start.15
  127.2 1.9 copy-start.16
  188.1 43.1 %all-to-all-start = ((bf16[192,8,1024]{2,0,1:T(8,128)(2,1)}), bf16[192,8,1024]{2,0,1:T(8,128)(2,1)}, u32[]{:S(2)}, u32[]{:S(2)}) async-start(bf16[192,8,1024]{2,0,1:T(8,128)(2,1)} %copy.63), calls=%async_computation | async-start | bytes 6291456 | tf_op jit(solution)/shard_map/all_to_all | solution.py:100
  207.4 4.2 %copy-start.19 = (bf16[16]{0:T(256)(128)(2,1)S(1)}, bf16[16]{0:T(256)(128)(2,1)}, u32[]{:S(2)}) copy-start(bf16[16]{0:T(256)(128)(2,1)} %reshape.263) | copy-start | bytes 100
  207.4 4.2 %copy-start.22 = (pred[16]{0:T(512)(128)(4,1)S(1)}, pred[16]{0:T(512)(128)(4,1)}, u32[]{:S(2)}) copy-start(pred[16]{0:T(512)(128)(4,1)} %compare_and_fusion.2) | copy-start | bytes 52
  228.3 7.5 %copy-start.7 = (s32[8,10]{1,0:T(8,128)S(1)}, s32[8,10]{1,0:T(8,128)}, u32[]{:S(2)}) copy-start(s32[8,10]{1,0:T(8,128)} %param.20) | copy-start | bytes 964
  228.3 7.5 %copy-start.13 = (pred[8,10]{1,0:T(8,128)(4,1)S(1)}, pred[8,10]{1,0:T(8,128)(4,1)}, u32[]{:S(2)}) copy-start(pred[8,10]{1,0:T(8,128)(4,1)} %get-tuple-element.52) | copy-start | bytes 244
  228.3 7.6 %copy-start.14 = (pred[8,10]{1,0:T(8,128)(4,1)S(1)}, pred[8,10]{1,0:T(8,128)(4,1)}, u32[]{:S(2)}) copy-start(pred[8,10]{1,0:T(8,128)(4,1)} %get-tuple-element.55) | copy-start | bytes 244
  228.3 7.8 %copy-start.9 = (s32[8,10]{1,0:T(8,128)S(1)}, s32[8,10]{1,0:T(8,128)}, u32[]{:S(2)}) copy-start(s32[8,10]{1,0:T(8,128)} %param.19) | copy-start | bytes 964
  231.2 42.9 %all-to-all-start.1 = ((bf16[192,8,1024]{2,0,1:T(8,128)(2,1)}), bf16[192,8,1024]{2,0,1:T(8,128)(2,1)}, u32[]{:S(2)}, u32[]{:S(2)}) async-start(bf16[192,8,1024]{2,0,1:T(8,128)(2,1)} %copy.73), calls=%async_computation.1 | async-start | bytes 6291456 | tf_op jit(solution)/shard_map/all_to_all | solution.py:121
  235.6 156.2 %reduce-scatter.7.cloned.1.call-start = ((), (), s32[]{:S(2)}) async-start(), calls=%async_computation.8 | async-start | bytes 8912896
  287.4 1.1 copy-start.1
  287.4 1.6 copy-start.3
  287.5 1.6 copy-start.11
  308.8 0.7 copy-start.10
Sparse Core Ops, SparseCore 0:
  16.3 43.3 all-gather.3
  61.9 40.9 all-gather.7
  105.0 56.5 all-gather.5
  164.9 78.7 reduce-scatter.4
  309.0 82.7 reduce-scatter.6
where the time goes:
time: 403 us; the launch traced here: 401 us
  waiting for transfers between devices  133 us (33%)
  local copies, waits for them, and re-layouts  113 us (28%)
  blocking collectives  72.9 us (18%)
  matrix products  35.7 us (9%)
  other arithmetic  23.6 us (6%)
  between operations  14.1 us (3%)
  starting transfers between devices  9.25 us (2%)
    psum x1, blocking collectives, on_device(): lax.psum((jnp.sum(grad_pre, axis=0), jnp.sum(grad_mixed, axis=0)), 'dp')  72.9 us
    all_gather x1, waiting for transfers between devices, on_device(): whole_start = lax.all_gather(start, 'tensor', axis=1, tiled=True)  38.5 us
    all_gather x1, waiting for transfers between devices, on_device(): whole_grad = lax.all_gather(grad_mixed_low, 'tensor', axis=1, tiled=True)  37 us
    all_to_all x1, waiting for transfers between devices, on_device(): lax.all_to_all(pack_parts(back_parts, chosen_in, filled_in), 'tensor', sp...  23.4 us
    all_gather x1, waiting for transfers between devices, on_device(): lax.all_gather(cross_blocks, 'dp', axis=1, tiled=True)  22.7 us
    reshape x4, local copies, waits for them, and re-layouts, pack_parts(): picked.reshape(parts.shape[0], chosen.shape[0], chosen.shape[1] * parts.s...  22.1 us
    unnamed x51, local copies, waits for them, and re-layouts  19.4 us
    reshape x2, local copies, waits for them, and re-layouts, collect_parts(): flattened = received.reshape(row_count, groups * capacity, block_width)  11.3 us
  transfers between devices with their start and end apart: 7, of which 6 were waited for; matrix products, arithmetic and copies ran while one was open for 39% of the time, Pallas kernels for 0%

commit v1 on v0

v1 whole, which is shorter than its diff:
```python
import jax
import jax.numpy as jnp
from jax import lax
from jax.sharding import PartitionSpec as P

BLK = 512
SLOTS = 10
CAP = 2


def slot_ranks(owner, alive):
    order = jnp.arange(owner.shape[1])
    earlier = order[None, :] < order[:, None]
    same = (owner[:, :, None] == owner[:, None, :]) & alive[:, None, :] & earlier[None, :, :]
    return jnp.sum(same.astype(jnp.int32), axis=2)


def send_table(owner, rank, alive, me, capacity):
    match = (
        (owner == me)[:, None, :]
        & alive[:, None, :]
        & (rank[:, None, :] == jnp.arange(capacity)[None, :, None])
    )
    chosen = jnp.sum(match.astype(jnp.int32) * jnp.arange(owner.shape[1])[None, None, :], axis=2)
    filled = jnp.any(match, axis=2)
    return chosen, filled


def pack_local(local_blocks, table_local, filled):
    rows = local_blocks.shape[0]
    picked = jnp.take(local_blocks, table_local.reshape(-1), axis=1)
    picked = picked * filled.reshape(-1)[None, :, None].astype(picked.dtype)
    return picked.reshape(rows, table_local.shape[0], table_local.shape[1] * BLK)


def pack_parts(parts, chosen, filled):
    picked = jnp.take(parts, chosen.reshape(-1), axis=1) * filled.reshape(-1)[None, :, None].astype(
        parts.dtype
    )
    return picked.reshape(parts.shape[0], chosen.shape[0], chosen.shape[1] * parts.shape[2])


def collect_parts(received, owner, local, rank, alive, target, capacity, per_device):
    row_count, groups, span_width = received.shape
    block_width = span_width // capacity
    match = ((owner == target) & alive)[:, :, None] & (
        rank[:, :, None] == jnp.arange(capacity)[None, None, :]
    )
    matches = match[:, :, :, None] & (
        local[:, :, None, None] == jnp.arange(per_device)[None, None, None, :]
    )
    onehot = (
        jnp.sum(matches.astype(jnp.int32), axis=1)
        .reshape(groups * capacity, per_device)
        .astype(jnp.bfloat16)
    )
    flattened = received.reshape(row_count, groups * capacity, block_width)
    summed = jnp.einsum("rib,il->rlb", flattened, onehot, preferred_element_type=jnp.float32)
    return summed.reshape(row_count, per_device * block_width)


def post_table(owner_mine, rank_mine, alive_mine, groups, capacity):
    match = (
        (owner_mine[None, None, :] == jnp.arange(groups)[:, None, None])
        & (rank_mine[None, None, :] == jnp.arange(capacity)[None, :, None])
        & alive_mine[None, None, :]
    )
    chosen = jnp.sum(match.astype(jnp.int32) * jnp.arange(owner_mine.shape[0])[None, None, :], axis=2)
    filled = jnp.any(match, axis=2)
    return (chosen, filled)


def on_device(
    dense,
    bottom_weight,
    bottom_bias,
    cross_blocks,
    cross_bias,
    cotangent,
    in_blocks,
    out_blocks,
    live_slots,
):
    groups = lax.axis_size("tensor")
    mine = lax.axis_index("tensor")
    row_count = dense.shape[0]
    local_width = bottom_weight.shape[1]
    per_device = local_width // BLK
    capacity = CAP
    weights = lax.all_gather(cross_blocks, "dp", axis=1, tiled=True)
    preact = jnp.dot(dense, bottom_weight, preferred_element_type=jnp.float32) + bottom_bias
    start = jax.nn.silu(preact).astype(jnp.bfloat16)
    start_wide = start.astype(jnp.float32)
    cot_wide = cotangent.astype(jnp.float32)
    grad_mixed = cot_wide * start_wide
    grad_mixed_low = grad_mixed.astype(jnp.bfloat16)
    grad_bias = lax.psum(jnp.sum(grad_mixed, axis=0), "dp")
    alive = jnp.arange(SLOTS)[None, :] < live_slots[:, None]
    alive_mine = alive[mine]
    switch = alive_mine.astype(jnp.bfloat16)[None, :, None]
    in_owner = in_blocks // per_device
    in_local = in_blocks % per_device
    out_owner = out_blocks // per_device
    out_local = out_blocks % per_device
    in_rank = slot_ranks(in_owner, alive)
    out_rank = slot_ranks(out_owner, alive)
    in_chosen, in_filled = send_table(in_owner, in_rank, alive, mine, capacity)
    out_chosen, out_filled = send_table(out_owner, out_rank, alive, mine, capacity)
    in_pick = jnp.take_along_axis(in_local, in_chosen.reshape(groups, -1), axis=1)
    out_pick = jnp.take_along_axis(out_local, out_chosen.reshape(groups, -1), axis=1)
    outgoing = jnp.concatenate(
        [
            pack_local(start.reshape(row_count, per_device, BLK), in_pick, in_filled),
            pack_local(grad_mixed_low.reshape(row_count, per_device, BLK), out_pick, out_filled),
        ],
        axis=2,
    )
    arrived = lax.all_to_all(outgoing, "tensor", split_axis=1, concat_axis=1, tiled=True)
    arrived = arrived.reshape(row_count, groups * 2 * capacity, BLK)
    in_index = in_owner[mine] * (2 * capacity) + jnp.minimum(in_rank[mine], capacity - 1)
    out_index = out_owner[mine] * (2 * capacity) + capacity + jnp.minimum(out_rank[mine], capacity - 1)
    fetched = jnp.take(arrived, in_index, axis=1) * switch
    upstream = jnp.take(arrived, out_index, axis=1) * switch
    block_terms = jnp.einsum("rki,rkj->kij", fetched, upstream, preferred_element_type=jnp.float32)
    grad_blocks = lax.psum_scatter(
        block_terms.astype(jnp.bfloat16), "dp", scatter_dimension=1, tiled=True
    ).astype(jnp.float32)
    product = jnp.einsum("rki,kij->rkj", fetched, weights, preferred_element_type=jnp.float32)
    parts = product.astype(jnp.bfloat16) * switch
    backward = jnp.einsum("rkj,kij->rki", upstream, weights, preferred_element_type=jnp.float32)
    back_parts = backward.astype(jnp.bfloat16) * switch
    chosen_out, filled_out = post_table(out_owner[mine], out_rank[mine], alive_mine, groups, capacity)
    chosen_in, filled_in = post_table(in_owner[mine], in_rank[mine], alive_mine, groups, capacity)
    returned = lax.all_to_all(
        jnp.concatenate(
            [
                pack_parts(parts, chosen_out, filled_out),
                pack_parts(back_parts, chosen_in, filled_in),
            ],
            axis=2,
        ),
        "tensor",
        split_axis=1,
        concat_axis=1,
        tiled=True,
    )
    arrived_parts = returned[:, :, : capacity * BLK]
    arrived_back = returned[:, :, capacity * BLK :]
    mixed = (
        collect_parts(arrived_parts, out_owner, out_local, out_rank, alive, mine, capacity, per_device)
        + cross_bias
    )
    cross_out = (start_wide * mixed + start_wide).astype(jnp.bfloat16)
    grad_start = collect_parts(
        arrived_back, in_owner, in_local, in_rank, alive, mine, capacity, per_device
    )
    grad_start = grad_start + cot_wide * mixed + cot_wide
    sigma = jax.nn.sigmoid(preact)
    grad_pre = grad_start * sigma * (1.0 + preact * (1.0 - sigma))
    grad_pre_low = grad_pre.astype(jnp.bfloat16)
    grad_bottom = lax.psum_scatter(
        lax.dot_general(
            dense, grad_pre_low, (((0,), (0,)), ((), ())), preferred_element_type=jnp.float32
        ).astype(jnp.bfloat16),
        "dp",
        scatter_dimension=0,
        tiled=True,
    ).astype(jnp.float32)
    grad_bias_bottom = lax.psum(jnp.sum(grad_pre, axis=0), "dp")
    return (cross_out, grad_bottom, grad_bias_bottom, grad_blocks, grad_bias)


def solution(mesh):
    return jax.shard_map(
        on_device,
        mesh=mesh,
        in_specs=(
            P("dp", None),
            P(None, "tensor"),
            P("tensor"),
            P("tensor", "dp", None),
            P("tensor"),
            P("dp", "tensor"),
            P(),
            P(),
            P(),
        ),
        out_specs=(
            P("dp", "tensor"),
            P("dp", "tensor"),
            P("tensor"),
            P("tensor", "dp", None),
            P("tensor"),
        ),
        check_vma=False,
    )
```

time: 403 us -> 463 us (1.15)
  local copies, waits for them, and re-layouts: 113 us -> 145 us
  waiting for transfers between devices: 133 us -> 150 us
    all_to_all x2, waiting for transfers between devices: 26.2 us -> 142 us  [the longest x1 71.4 us: on_device(): lax.all_to_all(jnp.concatenate([pack_parts(parts, chosen_out, filled_out)...]
    all_gather x3 -> x1, waiting for transfers between devices: 98.2 us -> 0.02 us  [on_device(): weights = lax.all_gather(cross_blocks, 'dp', axis=1, tiled=True)]
    reshape x2 -> x8, local copies, waits for them, and re-layouts: 12.5 us -> 31.7 us  [the longest x2 19.9 us: on_device(): arrived = arrived.reshape(row_count, groups * 2 * capacity, BLK)]
    slice x0 -> x3, local copies, waits for them, and re-layouts: none -> 12.3 us  [the longest x2 8.95 us: on_device(): arrived_back = returned[:, :, capacity * BLK:]]
    concatenate x0 -> x2, local copies, waits for them, and re-layouts: none -> 12.2 us  [the longest x1 6.11 us: on_device(): jnp.concatenate([pack_local(start.reshape(row_count, per_device, BLK), in...]
    reshape x4 -> x2, local copies, waits for them, and re-layouts: 22.1 us -> 11.8 us  [pack_parts(): picked.reshape(parts.shape[0], chosen.shape[0], chosen.shape[1] * parts.s...]
    gather x2 -> x14, local copies, waits for them, and re-layouts: 8.59 us -> 16.6 us  [the longest x1 4.92 us: on_device(): upstream = jnp.take(arrived, out_index, axis=1) * switch]
    concatenate x0 -> x2, other arithmetic: none -> 7.85 us  [the longest x1 3.93 us: on_device(): jnp.concatenate([pack_local(start.reshape(row_count, per_device, BLK), in...]
  transfers between devices with their start and end apart: 7 -> 5, of which waited for: 6 -> 3; matrix products, arithmetic and copies ran while one was open for 39% -> 45% of each run, Pallas kernels for 0% -> 0%
where the time goes in v1:
time: 463 us; the launch traced here: 457 us
  waiting for transfers between devices  150 us (32%)
  local copies, waits for them, and re-layouts  145 us (31%)
  blocking collectives  76.2 us (16%)
  matrix products  36.6 us (8%)
  other arithmetic  24.9 us (5%)
  between operations  14.3 us (3%)
  starting transfers between devices  9.63 us (2%)
    psum x1, blocking collectives, on_device(): grad_bias_bottom = lax.psum(jnp.sum(grad_pre, axis=0), 'dp')  76.2 us
    all_to_all x1, waiting for transfers between devices, on_device(): lax.all_to_all(jnp.concatenate([pack_parts(parts, chosen_out, filled_out)...  71.4 us
    all_to_all x1, waiting for transfers between devices, on_device(): lax.all_to_all(outgoing, 'tensor', split_axis=1, concat_axis=1, tiled=True)  70.5 us
    reshape x2, local copies, waits for them, and re-layouts, on_device(): arrived = arrived.reshape(row_count, groups * 2 * capacity, BLK)  19.9 us
    unnamed x19, local copies, waits for them, and re-layouts  16.1 us
    reshape x2, local copies, waits for them, and re-layouts, pack_parts(): picked.reshape(parts.shape[0], chosen.shape[0], chosen.shape[1] * parts.s...  11.8 us
    reshape x2, local copies, waits for them, and re-layouts, pack_local(): picked.reshape(rows, table_local.shape[0], table_local.shape[1] * BLK)  11.5 us
    reshape x2, local copies, waits for them, and re-layouts, collect_parts(): flattened = received.reshape(row_count, groups * capacity, block_width)  11.4 us
  transfers between devices with their start and end apart: 5, of which 3 were waited for; matrix products, arithmetic and copies ran while one was open for 45% of the time, Pallas kernels for 0%

profile of v1, /device:TPU:0, one launch (start us, length us, event | category | flops | bytes accessed | tf_op | source)
XLA Modules:
  0.0 456.7 jit_solution(13698828616667454102)
XLA Ops:
  14.0 6.7 %fusion.4 = (f32[2048]{0:T(1024)S(1)}, bf16[192,2048]{1,0:T(8,128)(2,1)S(1)}, f32[192,2048]{1,0:T(8,128)}) fusion(bf16[192,2048]{1,0:T(8,128)(2,1)S(1)} %copy-done.2, f32[2048]{0:T(1024)S(1)} %copy-done.6, bf16[192,2048]{1,0:T(8,128)(2,1)S(1)} %copy-done, bf16[2048,2048]{1,0:T(8,128)(2,1)} %param.18), kind=kOutput, calls=%fused_computation.31 | convolution fusion | flops 1614542848 | bytes 12337152 | tf_op jit(solution)/shard_map/dot_general | solution.py:91
  25.9 3.5 copy.121
  29.3 5.9 %reshape.303 = bf16[192,8,1024]{2,1,0:T(8,128)(2,1)} reshape(bf16[192,16,512]{2,1,0:T(8,128)(2,1)} %copy.121) | data formatting | bytes 6291456 | tf_op jit(solution)/shard_map/reshape | solution.py:33
  43.3 5.6 %reshape.300 = bf16[192,8,1024]{2,1,0:T(8,128)(2,1)} reshape(bf16[192,16,512]{2,1,0:T(8,128)(2,1)} %copy.114) | data formatting | bytes 6291456 | tf_op jit(solution)/shard_map/reshape | solution.py:33
  49.0 3.9 pad_maximum_fusion
  52.9 6.1 %copy.122 = bf16[192,8,2048]{2,0,1:T(8,128)(2,1)} copy(bf16[192,8,2048]{2,1,0:T(8,128)(2,1)S(1)} %pad_maximum_fusion) | data formatting | bytes 12582912 | tf_op jit(solution)/shard_map/concatenate | solution.py:111
  59.0 4.8 %all-to-all-start = ((bf16[192,8,2048]{2,0,1:T(8,128)(2,1)}), bf16[192,8,2048]{2,0,1:T(8,128)(2,1)}, u32[]{:S(2)}, u32[]{:S(2)}) async-start(bf16[192,8,2048]{2,0,1:T(8,128)(2,1)} %copy.122), calls=%async_computation | async-start | bytes 12582912 | tf_op jit(solution)/shard_map/all_to_all | solution.py:118
  65.4 70.5 %all-to-all-done = bf16[192,8,2048]{2,0,1:T(8,128)(2,1)} async-done(((bf16[192,8,2048]{2,0,1:T(8,128)(2,1)}), bf16[192,8,2048]{2,0,1:T(8,128)(2,1)}, u32[]{:S(2)}, u32[]{:S(2)}) %all-to-all-start) | async-done | bytes 6291488 | tf_op jit(solution)/shard_map/all_to_all | solution.py:118
  136.0 8.9 %copy.123 = bf16[192,8,2048]{2,1,0:T(8,128)(2,1)} copy(bf16[192,8,2048]{2,0,1:T(8,128)(2,1)} %all-to-all-done) | data formatting | bytes 12582912 | tf_op jit(solution)/shard_map/all_to_all | solution.py:118
  144.9 11.0 %reshape.304 = bf16[192,32,512]{2,1,0:T(8,128)(2,1)} reshape(bf16[192,8,2048]{2,1,0:T(8,128)(2,1)} %copy.123) | data formatting | bytes 12582912 | tf_op jit(solution)/shard_map/reshape | solution.py:119
  155.8 9.0 %copy.124 = bf16[192,32,512]{2,0,1:T(8,128)(2,1)} copy(bf16[192,32,512]{2,1,0:T(8,128)(2,1)} %reshape.304) | data formatting | bytes 12582912 | tf_op jit(solution)/shard_map/reshape | solution.py:119
  164.8 4.9 %gather_fusion.6 = bf16[10,192,512]{2,1,0:T(8,128)(2,1)} fusion(bf16[192,32,512]{2,0,1:T(8,128)(2,1)} %copy.124, s32[1024]{0:T(1024)S(1)} %pad_clamp_fusion.1), kind=kCustom, calls=%fused_computation.6.clone | custom fusion | bytes 3932200 | tf_op jit(solution)/shard_map/jit(_take)/gather | solution.py:123
  169.7 4.9 %gather_fusion.4 = bf16[10,192,512]{2,1,0:T(8,128)(2,1)} fusion(bf16[192,32,512]{2,0,1:T(8,128)(2,1)} %copy.124, s32[1024]{0:T(1024)S(1)} %pad_clamp_fusion.3), kind=kCustom, calls=%fused_computation.2.clone | custom fusion | bytes 3932200 | tf_op jit(solution)/shard_map/jit(_take)/gather | solution.py:122
  174.6 6.6 %convolution_convert_fusion = bf16[10,512,512]{2,1,0:T(8,128)(2,1)} fusion(bf16[10,192,512]{2,1,0:T(8,128)(2,1)} %gather_fusion.4, pred[10]{0:T(512)(128)(4,1)S(1)} %get-tuple-element.76, bf16[10]{0:T(256)(128)(2,1)S(1)} %get-tuple-element.59, bf16[10,192,512]{2,1,0:T(8,128)(2,1)} %gather_fusion.6, pred[10]{0:T(512)(128)(4,1)S(1)} %get-tuple-element.54), kind=kOutput, calls=%fused_computation.15 | convolution fusion | flops 1013186560 | bytes 9175080 | tf_op jit(solution)/shard_map/rki,rkj->kij/dot_general | solution.py:124
  181.3 6.3 %multiply_bitcast_fusion = bf16[192,10,512]{2,0,1:T(8,128)(2,1)} fusion(bf16[10,512,512]{2,1,0:T(8,128)(2,1)} %all-gather.2.cloned.1.call-done, bf16[10]{0:T(256)(128)(2,1)S(1)} %get-tuple-element.59, bf16[10,192,512]{2,1,0:T(8,128)(2,1)} %gather_fusion.6, pred[10]{0:T(512)(128)(4,1)S(1)} %get-tuple-element.54), kind=kOutput, calls=%fused_computation.23 | convolution fusion | flops 1010565120 | bytes 9175070 | tf_op jit(solution)/shard_map/rkj,kij->rki/dot_general | solution.py:130
  187.5 4.0 gather_fusion.7
  193.8 3.5 copy.130
  197.2 6.1 %reshape.308 = bf16[192,8,1024]{2,1,0:T(8,128)(2,1)} reshape(bf16[192,16,512]{2,1,0:T(8,128)(2,1)} %copy.130) | data formatting | bytes 6291456 | tf_op jit(solution)/shard_map/reshape | solution.py:40
  203.3 6.0 %multiply_bitcast_fusion.1 = bf16[192,10,512]{2,0,1:T(8,128)(2,1)} fusion(bf16[10,512,512]{2,1,0:T(8,128)(2,1)} %all-gather.2.cloned.1.call-done, bf16[10]{0:T(256)(128)(2,1)S(1)} %get-tuple-element.59, bf16[10,192,512]{2,1,0:T(8,128)(2,1)} %gather_fusion.4, pred[10]{0:T(512)(128)(4,1)S(1)} %get-tuple-element.76), kind=kOutput, calls=%fused_computation.24 | convolution fusion | flops 1010565120 | bytes 9175070 | tf_op jit(solution)/shard_map/rki,kij->rkj/dot_general | solution.py:128
  209.3 4.0 gather_fusion.5
  219.1 5.7 %reshape.306 = bf16[192,8,1024]{2,1,0:T(8,128)(2,1)} reshape(bf16[192,16,512]{2,1,0:T(8,128)(2,1)} %copy.126) | data formatting | bytes 6291456 | tf_op jit(solution)/shard_map/reshape | solution.py:40
  224.8 3.9 pad_maximum_fusion.1
  228.7 6.1 %copy.131 = bf16[192,8,2048]{2,0,1:T(8,128)(2,1)} copy(bf16[192,8,2048]{2,1,0:T(8,128)(2,1)S(1)} %pad_maximum_fusion.1) | data formatting | bytes 12582912 | tf_op jit(solution)/shard_map/concatenate | solution.py:135
  234.8 4.7 %all-to-all-start.1 = ((bf16[192,8,2048]{2,0,1:T(8,128)(2,1)}), bf16[192,8,2048]{2,0,1:T(8,128)(2,1)}, u32[]{:S(2)}, u32[]{:S(2)}) async-start(bf16[192,8,2048]{2,0,1:T(8,128)(2,1)} %copy.131), calls=%async_computation.1 | async-start | bytes 12582912 | tf_op jit(solution)/shard_map/all_to_all | solution.py:134
  240.3 71.4 %all-to-all-done.1 = bf16[192,8,2048]{2,0,1:T(8,128)(2,1)} async-done(((bf16[192,8,2048]{2,0,1:T(8,128)(2,1)}), bf16[192,8,2048]{2,0,1:T(8,128)(2,1)}, u32[]{:S(2)}, u32[]{:S(2)}) %all-to-all-start.1) | async-done | bytes 6291488 | tf_op jit(solution)/shard_map/all_to_all | solution.py:134
  311.7 5.6 %fusion.26 = (bf16[192,8,1024]{2,0,1:T(8,128)(2,1)S(1)}, bf16[192,8,1024]{2,0,1:T(8,128)(2,1)}) fusion(bf16[192,8,2048]{2,0,1:T(8,128)(2,1)} %all-to-all-done.1), kind=kLoop, calls=%fused_computation.118 | loop fusion | bytes 12582912 | tf_op jit(solution)/shard_map/slice | solution.py:148
  320.6 5.8 %reshape.311 = bf16[192,16,512]{2,1,0:T(8,128)(2,1)} reshape(bf16[192,8,1024]{2,1,0:T(8,128)(2,1)} %copy.136) | data formatting | bytes 6291456 | tf_op jit(solution)/shard_map/reshape | solution.py:57
  333.1 5.6 %reshape.309 = bf16[192,16,512]{2,1,0:T(8,128)(2,1)} reshape(bf16[192,8,1024]{2,1,0:T(8,128)(2,1)} %copy.132) | data formatting | bytes 6291456 | tf_op jit(solution)/shard_map/reshape | solution.py:57
  344.0 5.6 %convert_bitcast_fusion = bf16[2048,2048]{0,1:T(8,128)(2,1)} fusion(bf16[192,2048]{1,0:T(8,128)(2,1)S(1)} %copy-done, bf16[192,2048]{1,0:T(8,128)(2,1)S(1)} %get-tuple-element.50), kind=kOutput, calls=%fused_computation.8 | convolution fusion | flops 1614807040 | bytes 9961472 | tf_op jit(solution)/shard_map/dot_general | solution.py:162
  349.6 12.3 %copy.143 = bf16[2048,2048]{1,0:T(8,128)(2,1)} copy(bf16[2048,2048]{0,1:T(8,128)(2,1)} %convert_bitcast_fusion) | data formatting | bytes 16777216
  361.9 76.2 %all-reduce = (f32[2048]{0:T(1024)}, f32[2048]{0:T(1024)}) all-reduce(f32[2048]{0:T(1024)S(1)} %get-tuple-element.49, f32[2048]{0:T(1024)S(1)} %get-tuple-element.47), channel_id=1, replica_groups=mesh['dp'=16,'tensor'=8] {'dp'}, use_global_device_ids=true, to_apply=%region_14.19 | all-reduce | flops 4096 | bytes 32768 | tf_op jit(solution)/shard_map/psum | solution.py:169
  440.0 7.4 %reduce-scatter.7.cloned.1.call-done = bf16[128,2048]{1,0:T(8,128)(2,1)} async-done(((bf16[2048,2048]{1,0:T(8,128)(2,1)}), bf16[128,2048]{1,0:T(8,128)(2,1)}) %reduce-scatter.7.cloned.1.call-update) | async-done | bytes 524304
  (120 shorter events, 49.9 us)
Async XLA Ops:
  7.2 6.8 %copy-start = (bf16[192,2048]{1,0:T(8,128)(2,1)S(1)}, bf16[192,2048]{1,0:T(8,128)(2,1)}, u32[]{:S(2)}) copy-start(bf16[192,2048]{1,0:T(8,128)(2,1)} %param.17) | copy-start | bytes 2359300
  7.2 174.1 %all-gather.2.cloned.1.call-start = ((), (), s32[]{:S(2)}) async-start(), calls=%async_computation.4 | async-start | bytes 5570560 | tf_op jit(solution)/shard_map/all_gather | solution.py:90
  12.6 1.4 copy-start.2
  12.6 1.4 copy-start.6
  59.0 76.9 %all-to-all-start = ((bf16[192,8,2048]{2,0,1:T(8,128)(2,1)}), bf16[192,8,2048]{2,0,1:T(8,128)(2,1)}, u32[]{:S(2)}, u32[]{:S(2)}) async-start(bf16[192,8,2048]{2,0,1:T(8,128)(2,1)} %copy.122), calls=%async_computation | async-start | bytes 12582912 | tf_op jit(solution)/shard_map/all_to_all | solution.py:118
  63.8 374.3 %reduce-scatter.5.cloned.1.call-start = ((), (), s32[]{:S(2)}) async-start(), calls=%async_computation.5 | async-start | bytes 5570560 | tf_op jit(solution)/shard_map/reduce_scatter | solution.py:125
  234.8 76.9 %all-to-all-start.1 = ((bf16[192,8,2048]{2,0,1:T(8,128)(2,1)}), bf16[192,8,2048]{2,0,1:T(8,128)(2,1)}, u32[]{:S(2)}, u32[]{:S(2)}) async-start(bf16[192,8,2048]{2,0,1:T(8,128)(2,1)} %copy.131), calls=%async_computation.1 | async-start | bytes 12582912 | tf_op jit(solution)/shard_map/all_to_all | solution.py:134
  239.5 207.9 %reduce-scatter.7.cloned.1.call-start = ((), (), s32[]{:S(2)}) async-start(), calls=%async_computation.6 | async-start | bytes 8912896
  326.4 3.3 copy-start.1
  338.8 3.3 copy-start.3
  338.8 3.3 copy-start.4
  338.8 3.3 copy-start.5
Sparse Core Ops, SparseCore 0:
  10.2 58.9 all-gather.1
  181.3 79.7 reduce-scatter.4
  362.0 85.4 reduce-scatter.6
